TPU v7x, 256 devices: a whole 4x4x8 slice. The times are simulated.
256 devices in a mesh: seq: 64 (over y, z_hi, x, core), dp: 4 (over z_lo).
Axes of the slice: x: 4, y: 4, z: 8 (z_hi: 2, z_lo: 4; z = z_hi * 4 + z_lo), core: 2. Of those that a mesh axis runs over, the one named last changes fastest.
Arguments:
- inputs: bfloat16 [4, 64, 512, 512], P('dp', 'seq'), may hold values from -16 to 16
- norm_gain: float32 [512], replicated, may hold values from 0.25 to 1.75
- qkv_weight: bfloat16 [512, 1536], replicated, may hold values from -2 to 2
- out_weight: bfloat16 [512, 512], replicated, may hold values from -0.25 to 0.25
- out_cotan: bfloat16 [4, 64, 512, 512], P('dp', 'seq'), may hold values from -6 to 6
Outputs:
- input_grad: bfloat16 [4, 64, 512, 512], P('dp', 'seq')
- qkv_weight_grad: float32 [512, 1536], P('seq')
- out_weight_grad: float32 [512, 512], P('seq')
- gain_grad: float32 [512], P('seq')
All inputs are finite; a program needn't handle non-finite values.
Results may differ from a plain program's by a relative error of at most 0.0091.
Values may be sent and summed in bfloat16 or wider, within the bound.
A program may use at most 64 MiB of HBM per device.

v0:
```python
import math

import jax
import jax.numpy as jnp
from jax import lax
from jax.sharding import PartitionSpec as P

H = 8
HD = 64


def blocked(kernel, arrays, group_size):
    block_count = arrays[0].shape[0] // group_size
    split_arrays = tuple(
        (member.reshape((block_count, group_size) + member.shape[1:]) for member in arrays)
    )
    result = lax.map(lambda pieces: kernel(*pieces), split_arrays)
    return jax.tree.map(
        lambda member: member.reshape((block_count * group_size,) + member.shape[2:]), result
    )


def attend_probs(queries, key_vals):
    score_scale = HD ** (-0.5)
    scores = (
        jnp.einsum("glhd,gmhd->ghlm", queries, key_vals, preferred_element_type=jnp.float32)
        * score_scale
    )
    length = queries.shape[1]
    causal = lax.broadcasted_iota(jnp.int32, (length, length), 0) >= lax.broadcasted_iota(
        jnp.int32, (length, length), 1
    )
    scores = jnp.where(causal, scores, -1e30)
    row_max = jnp.max(scores, -1, keepdims=True)
    exponent = jnp.exp(scores - row_max)
    return exponent / jnp.sum(exponent, -1, keepdims=True)


def forward_block(queries, key_vals, values):
    weights = attend_probs(queries, key_vals).astype(jnp.bfloat16)
    return jnp.einsum(
        "ghlm,gmhd->glhd", weights, values, preferred_element_type=jnp.float32
    ).astype(jnp.bfloat16)


def backward_block(queries, key_vals, values, attended, cotangent):
    score_scale = HD ** (-0.5)
    softmax_probs = attend_probs(queries, key_vals)
    weights = softmax_probs.astype(jnp.bfloat16)
    prob_grad = jnp.einsum("glhd,gmhd->ghlm", cotangent, values, preferred_element_type=jnp.float32)
    row_delta = jnp.sum(cotangent.astype(jnp.float32) * attended.astype(jnp.float32), -1)
    row_delta = jnp.transpose(row_delta, (0, 2, 1))[..., None]
    score_grad = (softmax_probs * (prob_grad - row_delta)).astype(jnp.bfloat16)
    grad_query = (
        jnp.einsum("ghlm,gmhd->glhd", score_grad, key_vals, preferred_element_type=jnp.float32)
        * score_scale
    ).astype(jnp.bfloat16)
    grad_keys = (
        jnp.einsum("ghlm,glhd->gmhd", score_grad, queries, preferred_element_type=jnp.float32)
        * score_scale
    ).astype(jnp.bfloat16)
    grad_values = jnp.einsum(
        "ghlm,glhd->gmhd", weights, cotangent, preferred_element_type=jnp.float32
    ).astype(jnp.bfloat16)
    return (grad_query, grad_keys, grad_values)


def body(inputs, norm_gain, qkv_weight, out_weight, out_cotan):
    band_rows = inputs.shape[1]
    columns = inputs.shape[2]
    feature_width = inputs.shape[3]
    seq_count = lax.axis_size("seq")
    all_rows = band_rows * seq_count
    col_share = columns // seq_count
    half_heads = H // 2
    half_width = half_heads * HD
    tokens = band_rows * columns
    flat_input = inputs.reshape(tokens, feature_width).astype(jnp.float32)
    inverse_rms = lax.rsqrt(jnp.mean(flat_input * flat_input, -1, keepdims=True) + 1e-05)
    normed = flat_input * inverse_rms
    hidden = (normed * norm_gain).astype(jnp.bfloat16)
    weight_parts = qkv_weight.reshape(feature_width, 3, H, HD)
    weight_rows = weight_parts[:, :, :half_heads].reshape(feature_width, 3 * half_width)
    weight_cols = weight_parts[:, :, half_heads:].reshape(feature_width, 3 * half_width)
    row_proj = jnp.dot(hidden, weight_rows, preferred_element_type=jnp.float32).astype(jnp.bfloat16)
    row_grid = row_proj.reshape(band_rows, columns, 3, half_heads, HD)
    flat_cotan = out_cotan.reshape(tokens, feature_width)
    grad_att = jnp.dot(flat_cotan, out_weight.T, preferred_element_type=jnp.float32).astype(
        jnp.bfloat16
    )
    att_cot_grid = grad_att.reshape(band_rows, columns, H, HD)
    col_cot = att_cot_grid[:, :, half_heads:].reshape(band_rows, columns, half_width)
    col_group = math.gcd(col_share, max(1, 512 // all_rows))
    col_qkv = (
        jnp.dot(hidden, weight_cols, preferred_element_type=jnp.float32)
        .astype(jnp.bfloat16)
        .reshape(band_rows, columns, 3 * half_width)
    )
    received = lax.all_to_all(col_qkv, "seq", split_axis=1, concat_axis=0, tiled=True)
    col_grid = jnp.swapaxes(received, 0, 1).reshape(col_share, all_rows, 3, half_heads, HD)
    cols_in = (col_grid[:, :, 0], col_grid[:, :, 1], col_grid[:, :, 2])
    col_att = blocked(forward_block, cols_in, col_group)
    sent_att = jnp.swapaxes(col_att, 0, 1).reshape(all_rows, col_share, half_width)
    col_out = lax.all_to_all(sent_att, "seq", split_axis=0, concat_axis=1, tiled=True)
    received_cot = lax.all_to_all(col_cot, "seq", split_axis=1, concat_axis=0, tiled=True)
    cot_grid = jnp.swapaxes(received_cot, 0, 1).reshape(col_share, all_rows, half_heads, HD)
    col_grads = blocked(backward_block, cols_in + (col_att, cot_grid), col_group)
    stacked = jnp.swapaxes(jnp.stack(col_grads, 2), 0, 1).reshape(
        all_rows, col_share, 3 * half_width
    )
    col_dqkv = lax.all_to_all(stacked, "seq", split_axis=0, concat_axis=1, tiled=True)
    row_group = math.gcd(band_rows, max(1, 512 // columns))
    rows_in = (row_grid[:, :, 0], row_grid[:, :, 1], row_grid[:, :, 2])
    row_att = blocked(forward_block, rows_in, row_group)
    row_grads = blocked(
        backward_block, rows_in + (row_att, att_cot_grid[:, :, :half_heads]), row_group
    )
    attended = jnp.concatenate(
        [row_att, col_out.reshape(band_rows, columns, half_heads, HD)], 2
    ).reshape(tokens, feature_width)
    row_dqkv = jnp.stack(row_grads, 2)
    grad_qkv = jnp.concatenate(
        [row_dqkv, col_dqkv.reshape(band_rows, columns, 3, half_heads, HD)], 3
    ).reshape(tokens, 3 * feature_width)
    term_out = jnp.dot(attended.T, flat_cotan, preferred_element_type=jnp.float32)
    term_qkv = jnp.dot(hidden.T, grad_qkv, preferred_element_type=jnp.float32)
    grad_hidden = jnp.dot(grad_qkv, qkv_weight.T, preferred_element_type=jnp.float32)
    term_gain = jnp.sum(grad_hidden * normed, 0)
    grad_normed = grad_hidden * norm_gain
    grad_input = inverse_rms * (
        grad_normed - normed * jnp.mean(grad_normed * normed, -1, keepdims=True)
    )
    input_grad = (
        (flat_cotan.astype(jnp.float32) + grad_input).astype(jnp.bfloat16).reshape(inputs.shape)
    )
    full_qkv, full_out, full_gain = lax.psum((term_qkv, term_out, term_gain), ("seq", "dp"))
    row_share = feature_width // seq_count
    first_row = lax.axis_index("seq") * row_share
    sum_qkv = lax.dynamic_slice_in_dim(full_qkv, first_row, row_share, 0)
    sum_out = lax.dynamic_slice_in_dim(full_out, first_row, row_share, 0)
    sum_gain = lax.dynamic_slice_in_dim(full_gain, first_row, row_share, 0)
    return (input_grad, sum_qkv, sum_out, sum_gain)


def solution(mesh):
    return jax.shard_map(
        body,
        mesh=mesh,
        in_specs=(P("dp", "seq", None, None), P(), P(), P(), P("dp", "seq", None, None)),
        out_specs=(P("dp", "seq", None, None), P("seq", None), P("seq", None), P("seq")),
        check_vma=False,
    )
```

profile of v0, /device:TPU:1, one launch (start us, length us, event | category | flops | bytes accessed | tf_op | source)
XLA Modules:
  0.0 444.6 jit_solution(2909566753671628092)
XLA Ops:
  8.2 1.5 convolution_convert_fusion.4
  11.5 2.2 reduce.5
  14.6 15.8 %all-to-all-start.1 = ((bf16[64,2,1024]{2,1,0:T(2,128)(2,1)}), bf16[64,2,1024]{2,1,0:T(2,128)(2,1)}, u32[]{:S(2)}, u32[]{:S(2)}) async-start(bf16[64,2,1024]{2,1,0:T(2,128)(2,1)} %reshape.245), calls=%async_computation.1 | async-start | bytes 524288 | tf_op jit(solution)/shard_map/all_to_all | solution.py:105
  30.6 1.7 copy.93
  32.3 1.0 fusion.60
  34.0 1.2 copy.168
  35.2 5.4 %reduce.6 = bf16[512,768]{1,0:T(8,128)(2,1)S(1)} reduce(bf16[512,1,768]{2,1,0:T(2,128)(2,1)S(1)} %bitcast.188, bf16[]{:T(256)} %broadcast.106), dimensions={1}, to_apply=%bitcast.186.reduce_sub_computation | reduce | bytes 1572866
  40.6 1.2 reshape.247
  41.8 2.2 all-to-all-done.1
  44.0 10.7 %all-to-all-start = ((bf16[64,2,3072]{2,1,0:T(2,128)(2,1)}), bf16[64,2,3072]{2,1,0:T(2,128)(2,1)}, u32[]{:S(2)}, u32[]{:S(2)}) async-start(bf16[64,2,3072]{2,1,0:T(2,128)(2,1)} %reshape.247), calls=%async_computation | async-start | bytes 1572864 | tf_op jit(solution)/shard_map/all_to_all | solution.py:99
  55.8 3.6 fusion.63
  59.4 2.8 fusion.6
  62.3 2.1 multiply_reduce_fusion
  64.4 2.8 reshape.246
  67.2 1.1 copy.167
  68.3 1.1 copy.151
  69.3 7.4 %all-to-all-done = bf16[64,2,3072]{2,1,0:T(2,128)(2,1)} async-done(((bf16[64,2,3072]{2,1,0:T(2,128)(2,1)}), bf16[64,2,3072]{2,1,0:T(2,128)(2,1)}, u32[]{:S(2)}, u32[]{:S(2)}) %all-to-all-start) | async-done | bytes 786464 | tf_op jit(solution)/shard_map/all_to_all | solution.py:99
  76.7 5.8 %reshape.248 = bf16[512,1,768]{2,1,0:T(2,128)(2,1)} reshape(bf16[64,2,3072]{2,1,0:T(2,128)(2,1)} %all-to-all-done) | data formatting | bytes 1572864
  82.5 2.4 copy.166
  84.9 3.5 reshape.243
  88.4 2.7 fusion.61
  91.6 1.3 fusion.62
  93.0 3.3 fusion.38
  96.2 2.0 copy.141
  98.2 7.6 %all-to-all-start.3 = ((bf16[64,8,256]{2,1,0:T(8,128)(2,1)}), bf16[64,8,256]{2,1,0:T(8,128)(2,1)S(1)}, u32[]{:S(2)}, u32[]{:S(2)}) async-start(bf16[64,8,256]{2,1,0:T(8,128)(2,1)} %copy.141), calls=%async_computation.3 | async-start | bytes 524288 | tf_op jit(solution)/shard_map/all_to_all | solution.py:104
  105.8 2.7 fusion.16
  108.6 3.0 fusion.22
  111.5 1.6 fusion.21
  113.2 1.5 fusion.20
  115.1 2.4 copy.121
  117.5 3.6 reshape.235
  121.1 12.9 %all-to-all-start.2 = ((bf16[64,8,768]{2,1,0:T(8,128)(2,1)}), bf16[64,8,768]{2,1,0:T(8,128)(2,1)}, u32[]{:S(2)}, u32[]{:S(2)}) async-start(bf16[64,8,768]{2,1,0:T(8,128)(2,1)} %reshape.235), calls=%async_computation.2 | async-start | bytes 1572864 | tf_op jit(solution)/shard_map/all_to_all | solution.py:111
  134.1 1.8 fusion.28
  135.9 2.9 multiply_convert_fusion
  138.9 1.5 fusion.25
  140.4 1.2 fusion.26
  142.2 1.4 fusion.41
  143.6 13.3 %all-to-all-done.2 = bf16[64,8,768]{2,1,0:T(8,128)(2,1)} async-done(((bf16[64,8,768]{2,1,0:T(8,128)(2,1)}), bf16[64,8,768]{2,1,0:T(8,128)(2,1)}, u32[]{:S(2)}, u32[]{:S(2)}) %all-to-all-start.2) | async-done | bytes 786464 | tf_op jit(solution)/shard_map/all_to_all | solution.py:111
  156.9 2.8 reshape.236
  159.7 2.3 copy.122
  162.0 1.4 pad_maximum_fusion
  163.4 2.9 fusion.54
  166.3 3.6 fusion.34
  170.0 78.7 %psum.23 = f32[512]{0:T(512)S(1)} all-reduce(f32[512]{0:T(512)S(1)} %get-tuple-element.60), channel_id=1, replica_groups=mesh['seq'=64,'dp'=4] {'seq','dp'}, use_global_device_ids=true, to_apply=%region_11.12 | all-reduce | flops 512 | bytes 4096 | tf_op jit(solution)/shard_map/psum | solution.py:136
  249.3 2.4 fusion.40
  251.7 183.3 %all-reduce.3.cloned.1.call-done = (f32[512,1536]{1,0:T(8,128)}, f32[512,512]{1,0:T(8,128)}) async-done(((f32[512,1536]{1,0:T(8,128)}, f32[512,512]{1,0:T(8,128)}), (f32[512,1536]{1,0:T(8,128)}, f32[512,512]{1,0:T(8,128)})) %all-reduce.3.cloned.1.call-update) | async-done | bytes 4194320 | tf_op jit(solution)/shard_map/psum | solution.py:136
  435.0 1.4 constant_dynamic-slice_fusion.1
  436.4 1.3 constant_dynamic-slice_fusion
  (55 shorter events, 7.6 us)
Async XLA Ops:
  7.2 1.0 copy-start
  7.2 23.2 %copy-start.1 = (bf16[1,1,512,512]{3,2,1,0:T(8,128)(2,1)S(1)}, bf16[1,1,512,512]{3,2,1,0:T(8,128)(2,1)}, u32[]{:S(2)}) copy-start(bf16[1,1,512,512]{3,2,1,0:T(8,128)(2,1)} %param.5) | copy-start | bytes 1572868
  9.7 0.8 copy-start.3
  14.6 29.5 %all-to-all-start.1 = ((bf16[64,2,1024]{2,1,0:T(2,128)(2,1)}), bf16[64,2,1024]{2,1,0:T(2,128)(2,1)}, u32[]{:S(2)}, u32[]{:S(2)}) async-start(bf16[64,2,1024]{2,1,0:T(2,128)(2,1)} %reshape.245), calls=%async_computation.1 | async-start | bytes 524288 | tf_op jit(solution)/shard_map/all_to_all | solution.py:105
  32.3 1.0 copy-start.16
  40.6 14.1 %copy-start.14 = (bf16[512,3,4,64]{0,3,2,1:T(8,128)(2,1)S(1)}, bf16[512,3,4,64]{0,3,2,1:T(8,128)(2,1)}, u32[]{:S(2)}) copy-start(bf16[512,3,4,64]{0,3,2,1:T(8,128)(2,1)} %get-tuple-element.69) | copy-start | bytes 2359300
  44.0 32.7 %all-to-all-start = ((bf16[64,2,3072]{2,1,0:T(2,128)(2,1)}), bf16[64,2,3072]{2,1,0:T(2,128)(2,1)}, u32[]{:S(2)}, u32[]{:S(2)}) async-start(bf16[64,2,3072]{2,1,0:T(2,128)(2,1)} %reshape.247), calls=%async_computation | async-start | bytes 1572864 | tf_op jit(solution)/shard_map/all_to_all | solution.py:99
  55.7 3.7 copy-start.6
  59.4 2.8 copy-start.4
  91.1 1.8 copy-start.8
  91.1 1.8 copy-start.9
  91.6 1.3 copy-start.12
  98.2 22.9 %all-to-all-start.3 = ((bf16[64,8,256]{2,1,0:T(8,128)(2,1)}), bf16[64,8,256]{2,1,0:T(8,128)(2,1)S(1)}, u32[]{:S(2)}, u32[]{:S(2)}) async-start(bf16[64,8,256]{2,1,0:T(8,128)(2,1)} %copy.141), calls=%async_computation.3 | async-start | bytes 524288 | tf_op jit(solution)/shard_map/all_to_all | solution.py:104
  111.5 3.2 copy-start.15
  121.1 12.9 %copy-start.10 = (bf16[64,8,256]{2,1,0:T(8,128)(2,1)}, bf16[64,8,256]{2,1,0:T(8,128)(2,1)S(1)}, u32[]{:S(2)}) copy-start(bf16[64,8,256]{2,1,0:T(8,128)(2,1)S(1)} %all-to-all-done.3) | copy-start | bytes 786436
  121.1 35.8 %all-to-all-start.2 = ((bf16[64,8,768]{2,1,0:T(8,128)(2,1)}), bf16[64,8,768]{2,1,0:T(8,128)(2,1)}, u32[]{:S(2)}, u32[]{:S(2)}) async-start(bf16[64,8,768]{2,1,0:T(8,128)(2,1)} %reshape.235), calls=%async_computation.2 | async-start | bytes 1572864 | tf_op jit(solution)/shard_map/all_to_all | solution.py:111
  134.0 300.9 %all-reduce.3.cloned.1.call-start = ((), (), s32[]{:S(2)}) async-start(), calls=%async_computation.4 | async-start | bytes 8388608 | tf_op jit(solution)/shard_map/psum | solution.py:136
  134.1 1.8 copy-start.5
  134.1 1.8 copy-start.7
  138.9 2.7 copy-start.11
  140.4 1.8 copy-start.13
  140.4 1.8 copy-start.2
Sparse Core Ops, SparseCore 0:
  166.4 268.4 all-reduce.2
where the time goes:
time: 447 us; the launch traced here: 445 us
  waiting for transfers between devices  206 us (46%)
  blocking collectives  78.7 us (18%)
  starting transfers between devices  47 us (11%)
  local copies, waits for them, and re-layouts  45.3 us (10%)
  matrix products  36.5 us (8%)
  other arithmetic  16.3 us (4%)
  between operations  14.4 us (3%)
    psum x1, waiting for transfers between devices, body(): lax.psum((term_qkv, term_out, term_gain), ('seq', 'dp'))  183 us
    psum x1, blocking collectives, body(): lax.psum((term_qkv, term_out, term_gain), ('seq', 'dp'))  78.7 us
    unnamed x42, local copies, waits for them, and re-layouts  18.2 us
    all_to_all x1, starting transfers between devices, body(): lax.all_to_all(col_cot, 'seq', split_axis=1, concat_axis=0, tiled=True)  15.8 us
    all_to_all x1, waiting for transfers between devices, body(): lax.all_to_all(stacked, 'seq', split_axis=0, concat_axis=1, tiled=True)  13.3 us
    all_to_all x1, starting transfers between devices, body(): lax.all_to_all(stacked, 'seq', split_axis=0, concat_axis=1, tiled=True)  12.9 us
    all_to_all x1, starting transfers between devices, body(): lax.all_to_all(col_qkv, 'seq', split_axis=1, concat_axis=0, tiled=True)  10.7 us
  transfers between devices with their start and end apart: 5, of which 4 were waited for; matrix products, arithmetic and copies ran while one was open for 13% of the time, Pallas kernels for 0%

commit v1 on v0

v1 whole, which is shorter than its diff:
```python
import jax
import jax.numpy as jnp
from jax import lax
from jax.experimental import pallas as pl
from jax.experimental.pallas import tpu as pltpu
from jax.sharding import PartitionSpec as P

MESH = pl.DeviceIdType.MESH
BF = jnp.bfloat16
F32 = jnp.float32
TOK = 512
D = 512
HALF = 256
HD = 64
RANKS = 64
LINE = 4
NC = 2048 + 128
CH = 128


def dot(a, b, ca, cb):
    return lax.dot_general(a, b, (((ca,), (cb,)), ((), ())), preferred_element_type=F32)


def rows8(ref, i):
    return ref[pl.ds(i * (CH // 8), CH // 8)].astype(F32).reshape(CH, D)


def norm_of(x):
    inv = lax.rsqrt(jnp.mean(x * x, -1, keepdims=True) + 1e-05)
    return inv, x * inv


def prepare(x_ref, c_ref, g_ref, hid_t, cot):
    def step(i, carry):
        x = rows8(x_ref, i)
        _, normed = norm_of(x)
        at = pl.multiple_of(i * CH, CH)
        hid_t[:, pl.ds(at, CH)] = (normed * g_ref[...]).T.astype(BF)
        cot[pl.ds(at, CH), :] = rows8(c_ref, i).astype(BF)
        return carry

    lax.fori_loop(0, TOK // CH, step, 0)


def project(w_ref, wo_ref, off, hid_t, cot, qkv_t, ga_t):
    for part in range(3):
        p = dot(w_ref[:, part * D + off : part * D + off + HALF], hid_t[...], 0, 0).astype(BF)
        if part == 0:
            p = p * BF(HD**-0.5)
        qkv_t[part * HALF : (part + 1) * HALF, :] = p
    ga_t[...] = dot(wo_ref[off : off + HALF, :], cot[...], 1, 1).astype(BF)


def attend(is_col, qkv_t, ga_t, att_t, d_t):
    qb = TOK // 2

    def head(h, carry):
        at = pl.multiple_of(h * HD, HD)
        sl = pl.ds(at, HD)
        dk = dv = None
        for b in range(2):
            kl = qb * (b + 1)
            qs = slice(b * qb, (b + 1) * qb)
            q = qkv_t[sl, qs]
            k = qkv_t[pl.ds(HALF + at, HD), :kl]
            v = qkv_t[pl.ds(2 * HALF + at, HD), :kl]
            ga = ga_t[sl, qs]
            s = dot(k, q, 0, 0)
            gap = (
                lax.broadcasted_iota(jnp.int32, (kl, qb), 1)
                + b * qb
                - lax.broadcasted_iota(jnp.int32, (kl, qb), 0)
            )
            allowed = gap >= 0
            if is_col:
                allowed = jnp.logical_and(allowed, jnp.bitwise_and(gap, 7) == 0)
            s = jnp.where(allowed, s, -1e30)
            e = jnp.exp(s - jnp.max(s, 0, keepdims=True))
            p = e * (1.0 / jnp.sum(e, 0, keepdims=True))
            w = p.astype(BF)
            o = dot(v, w, 1, 0).astype(BF)
            att_t[sl, qs] = o
            dp = dot(v, ga, 0, 0)
            delta = jnp.sum(ga.astype(F32) * o.astype(F32), 0, keepdims=True)
            ds = (p * (dp - delta)).astype(BF)
            d_t[sl, qs] = (dot(k, ds, 1, 0) * (HD**-0.5)).astype(BF)
            dkb, dvb = dot(q, ds, 1, 1), dot(ga, w, 1, 1)
            if b == 0:
                dk, dv = dkb, dvb
            else:
                dk = jnp.concatenate([dk + dkb[:, :qb], dkb[:, qb:]], 1)
                dv = jnp.concatenate([dv + dvb[:, :qb], dvb[:, qb:]], 1)
        d_t[pl.ds(HALF + at, HD), :] = dk.astype(BF)
        d_t[pl.ds(2 * HALF + at, HD), :] = dv.astype(BF)
        return carry

    lax.fori_loop(0, HALF // HD, head, 0)


def hidden_grad(w_ref, off, d_t, dh):
    for part in range(3):
        d = d_t[part * HALF : (part + 1) * HALF, :]
        term = dot(d, w_ref[:, part * D + off : part * D + off + HALF], 0, 1)
        if part == 0:
            dh[...] = term
        else:
            dh[...] += term


def weight_grads(off, base, hid_t, cot, att_t, d_t, terms):
    for part in range(3):
        d = d_t[part * HALF : (part + 1) * HALF, :]
        at = base + part * HALF
        terms[:, :, at : at + HALF] = dot(hid_t[...], d, 1, 1).reshape(RANKS, 8, HALF)
    half = slice(off // 8, (off + HALF) // 8)
    terms[half, :, 3 * D : 4 * D] = dot(att_t[...], cot[...], 1, 0).reshape(HALF // 8, 8, D)


def gain_term(x_ref, dh):
    def step(i, total):
        _, normed = norm_of(rows8(x_ref, i))
        at = pl.multiple_of(i * CH, CH)
        return total + jnp.sum(dh[pl.ds(at, CH), :] * normed, 0, keepdims=True)

    return lax.fori_loop(0, TOK // CH, step, jnp.zeros((1, D), F32))


def kernel(
    x_ref, c_ref, g_ref, w_ref, wo_ref,
    out_ref, gq_ref, go_ref, gg_ref,
    xr, cr, hid_t, cot, qkv_t, ga_t, att_t, d_t, dh_row, dh_col, dh_send, dh_recv,
    terms, core_send, core_recv, plane_send, plane_recv, z_sum, z_send, z_recv,
    send_sem, recv_sem, own_sem,
):
    me = lax.axis_index("seq")
    line = lax.axis_index("dp")
    core = me % 2
    z_hi = (me // 8) % 2
    plane = (me // 16) * 4 + (me // 2) % 4

    def rank_of(other, hi):
        return (other // 4) * 16 + hi * 8 + (other % 4) * 2 + core

    def remote(src, dst, i, target):
        return pltpu.make_async_remote_copy(
            src, dst, send_sem.at[i], recv_sem.at[i], device_id=target, device_id_type=MESH
        )

    def peer(t):
        return lax.rem(me + t, RANKS)

    def each_peer(f):
        def step(t, carry):
            f(peer(t))
            return carry

        lax.fori_loop(1, RANKS, step, 0)

    def each_line_peer(f):
        def step(t, carry):
            z = lax.rem(z_hi * LINE + line + t, 2 * LINE)
            f(z // LINE, z % LINE)
            return carry

        lax.fori_loop(1, 2 * LINE, step, 0)

    barrier = pltpu.get_barrier_semaphore()
    each_peer(lambda t: pl.semaphore_signal(barrier, inc=1, device_id={"seq": t}, device_id_type=MESH))
    for hi in range(2):
        for t in range(1, LINE):
            pl.semaphore_signal(
                barrier,
                inc=1,
                device_id={"seq": rank_of(plane, hi), "dp": lax.rem(line + t, LINE)},
                device_id_type=MESH,
            )
    pl.semaphore_wait(barrier, RANKS - 1 + 2 * (LINE - 1))

    def send_in(t):
        remote(x_ref.at[t], xr.at[me], 0, {"seq": t}).start()
        remote(c_ref.at[t], cr.at[me], 1, {"seq": t}).start()

    each_peer(send_in)
    own_x = pltpu.make_async_copy(x_ref.at[me], xr.at[me], own_sem.at[0])
    own_c = pltpu.make_async_copy(c_ref.at[me], cr.at[me], own_sem.at[1])
    own_x.start()
    own_c.start()

    prepare(x_ref, c_ref, g_ref, hid_t, cot)
    project(w_ref, wo_ref, 0, hid_t, cot, qkv_t, ga_t)
    attend(False, qkv_t, ga_t, att_t, d_t)
    hidden_grad(w_ref, 0, d_t, dh_row)
    weight_grads(0, 0, hid_t, cot, att_t, d_t, terms)
    gain_row = gain_term(x_ref, dh_row)

    own_x.wait()
    own_c.wait()
    rest = pl.ds(0, RANKS - 1)
    in_x = remote(x_ref.at[rest], xr.at[rest], 0, {"seq": me})
    in_c = remote(c_ref.at[rest], cr.at[rest], 1, {"seq": me})
    in_x.wait_recv()
    in_c.wait_recv()

    prepare(xr, cr, g_ref, hid_t, cot)
    project(w_ref, wo_ref, HALF, hid_t, cot, qkv_t, ga_t)
    attend(True, qkv_t, ga_t, att_t, d_t)
    hidden_grad(w_ref, HALF, d_t, dh_col)

    def round_out(i, carry):
        at = pl.multiple_of(i * CH, CH)
        dh_send[pl.ds(i * (CH // 8), CH // 8)] = dh_col[pl.ds(at, CH), :].reshape(CH // 8, 8, D).astype(BF)
        return carry

    lax.fori_loop(0, TOK // CH, round_out, 0)
    each_peer(lambda t: remote(dh_send.at[t], dh_recv.at[me], 2, {"seq": t}).start())
    own_h = pltpu.make_async_copy(dh_send.at[me], dh_recv.at[me], own_sem.at[0])
    own_h.start()

    weight_grads(HALF, 3 * HALF, hid_t, cot, att_t, d_t, terms)
    gain = gain_row + gain_term(xr, dh_col)
    terms[:, :, 4 * D :] = jnp.broadcast_to(gain, (128, D)).T.reshape(RANKS, 8, 128)

    def pack_core(b, carry):
        core_send[b] = terms[2 * b + 1 - core].astype(BF)
        return carry

    lax.fori_loop(0, RANKS // 2, pack_core, 0)
    pair = remote(core_send, core_recv, 3, {"seq": me + 1 - 2 * core})
    pair.start()
    pair.wait_recv()

    def pack_plane(b, carry):
        y, hi, x = b // 8, (b // 4) % 2, b % 4
        total = terms[2 * b + core] + core_recv[b].astype(F32)
        terms[2 * b + core] = total
        plane_send[y * 4 + x, hi] = total.astype(BF)
        return carry

    lax.fori_loop(0, RANKS // 2, pack_plane, 0)

    def send_plane(t, carry):
        other = lax.rem(plane + t, 16)
        remote(plane_send.at[other], plane_recv.at[plane], 4, {"seq": rank_of(other, z_hi)}).start()
        return carry

    lax.fori_loop(1, 16, send_plane, 0)

    own_h.wait()
    remote(dh_send.at[rest], dh_recv.at[rest], 2, {"seq": me}).wait_recv()

    def finish(i, carry):
        at = pl.multiple_of(i * CH, CH)
        inv, normed = norm_of(rows8(x_ref, i))
        grad_normed = (dh_row[pl.ds(at, CH), :] + rows8(dh_recv, i)) * g_ref[...]
        mean = jnp.mean(grad_normed * normed, -1, keepdims=True)
        grad = rows8(c_ref, i) + inv * (grad_normed - normed * mean)
        out_ref[pl.ds(i * (CH // 8), CH // 8)] = grad.astype(BF).reshape(CH // 8, 8, D)
        return carry

    lax.fori_loop(0, TOK // CH, finish, 0)

    pl_rest = pl.ds(0, 15)
    plane_in = remote(plane_send.at[pl_rest], plane_recv.at[pl_rest], 4, {"seq": me})
    plane_in.wait_recv()

    for hi in range(2):
        own_rank = (plane // 4) * 16 + hi * 8 + (plane % 4) * 2 + core
        z_sum[hi] = terms[own_rank]

        def add_plane(t, carry, hi=hi):
            other = lax.rem(plane + t, 16)
            z_sum[hi] += plane_recv[other, hi].astype(F32)
            return carry

        lax.fori_loop(1, 16, add_plane, 0)
        z_send[hi] = z_sum[hi].astype(BF)

    my_z = z_hi * LINE + line
    each_line_peer(
        lambda hi, lo: remote(
            z_send.at[hi], z_recv.at[my_z], 5, {"seq": rank_of(plane, hi), "dp": lo}
        ).start()
    )
    z_rest = pl.ds(0, 2 * LINE - 1)
    z_in = remote(z_recv.at[z_rest], z_recv.at[z_rest], 5, {"seq": me})
    z_in.wait_recv()
    z_sum[0] = z_sum[z_hi]

    def add_z(t, carry):
        z_sum[0] += z_recv[lax.rem(my_z + t, 2 * LINE)].astype(F32)
        return carry

    lax.fori_loop(1, 2 * LINE, add_z, 0)
    for part in range(3):
        gq_ref[:, part * D : part * D + HALF] = z_sum[0, :, part * HALF : (part + 1) * HALF]
        gq_ref[:, part * D + HALF : (part + 1) * D] = z_sum[0, :, (3 + part) * HALF : (4 + part) * HALF]
    go_ref[...] = z_sum[0, :, 3 * D : 4 * D]
    gg_ref[...] = z_sum[0, :, 4 * D :]

    in_x.wait_send()
    in_c.wait_send()
    remote(dh_send.at[rest], dh_recv.at[rest], 2, {"seq": me}).wait_send()
    pair.wait_send()
    plane_in.wait_send()
    z_in.wait_send()


def body(inputs, norm_gain, qkv_weight, out_weight, out_cotan):
    vmem = pl.BlockSpec(memory_space=pltpu.VMEM)
    grad, grad_qkv, grad_out, grad_gain = pl.pallas_call(
        kernel,
        out_shape=(
            jax.ShapeDtypeStruct((RANKS, 8, D), BF),
            jax.ShapeDtypeStruct((8, 3 * D), F32),
            jax.ShapeDtypeStruct((8, D), F32),
            jax.ShapeDtypeStruct((8, 128), F32),
        ),
        in_specs=[vmem] * 5,
        out_specs=(vmem,) * 4,
        scratch_shapes=[
            pltpu.VMEM((RANKS, 8, D), BF),
            pltpu.VMEM((RANKS, 8, D), BF),
            pltpu.VMEM((D, TOK), BF),
            pltpu.VMEM((TOK, D), BF),
            pltpu.VMEM((3 * HALF, TOK), BF),
            pltpu.VMEM((HALF, TOK), BF),
            pltpu.VMEM((HALF, TOK), BF),
            pltpu.VMEM((3 * HALF, TOK), BF),
            pltpu.VMEM((TOK, D), F32),
            pltpu.VMEM((TOK, D), F32),
            pltpu.VMEM((RANKS, 8, D), BF),
            pltpu.VMEM((RANKS, 8, D), BF),
            pltpu.VMEM((RANKS, 8, NC), F32),
            pltpu.VMEM((RANKS // 2, 8, NC), BF),
            pltpu.VMEM((RANKS // 2, 8, NC), BF),
            pltpu.VMEM((16, 2, 8, NC), BF),
            pltpu.VMEM((16, 2, 8, NC), BF),
            pltpu.VMEM((2, 8, NC), F32),
            pltpu.VMEM((2, 8, NC), BF),
            pltpu.VMEM((2 * LINE, 8, NC), BF),
            pltpu.SemaphoreType.DMA((6,)),
            pltpu.SemaphoreType.DMA((6,)),
            pltpu.SemaphoreType.DMA((2,)),
        ],
        compiler_params=pltpu.CompilerParams(
            collective_id=0, has_side_effects=True, vmem_limit_bytes=48 * 1024 * 1024
        ),
    )(
        inputs.reshape(RANKS, 8, D),
        out_cotan.reshape(RANKS, 8, D),
        norm_gain.reshape(1, D),
        qkv_weight,
        out_weight,
    )
    return (grad.reshape(inputs.shape), grad_qkv, grad_out, grad_gain[:, 0])


def solution(mesh):
    return jax.shard_map(
        body,
        mesh=mesh,
        in_specs=(P("dp", "seq", None, None), P(), P(), P(), P("dp", "seq", None, None)),
        out_specs=(P("dp", "seq", None, None), P("seq", None), P("seq", None), P("seq")),
        check_vma=False,
    )
```

time: 447 us -> 88.7 us (0.20)
  waiting for transfers between devices: 206 us -> 0 us
  Pallas kernels: 0 us -> 79.9 us
  blocking collectives: 78.7 us -> 0 us
  starting transfers between devices: 47 us -> 0 us
  local copies, waits for them, and re-layouts: 45.3 us -> 7.85 us
  matrix products: 36.5 us -> 0 us
  other arithmetic: 16.3 us -> 0 us
  between operations: 14.4 us -> 0.65 us
    psum x1 -> x0, waiting for transfers between devices: 183 us -> none  [body(): lax.psum((term_qkv, term_out, term_gain), ('seq', 'dp'))]
    pallas_call x0 -> x1, Pallas kernels: none -> 79.9 us  [body(): pl.pallas_call(kernel, out_shape=(jax.ShapeDtypeStruct((RANKS, 8, D), BF)...]
    psum x1 -> x0, blocking collectives: 78.7 us -> none  [body(): lax.psum((term_qkv, term_out, term_gain), ('seq', 'dp'))]
    all_to_all x4 -> x0, starting transfers between devices: 47 us -> none  [the longest x1 15.8 us: body(): lax.all_to_all(col_cot, 'seq', split_axis=1, concat_axis=0, tiled=True)]
    dot_general x17 -> x0, matrix products: 32.9 us -> none  [the longest x2 5.7 us: backward_block(): jnp.einsum('glhd,gmhd->ghlm', cotangent, values, preferred_element_type=j...]
    all_to_all x4 -> x0, waiting for transfers between devices: 22.9 us -> none  [the longest x1 13.3 us: body(): lax.all_to_all(stacked, 'seq', split_axis=0, concat_axis=1, tiled=True)]
    reshape x9 -> x0, local copies, waits for them, and re-layouts: 16.3 us -> none  [the longest x2 5.05 us: body(): col_dqkv.reshape(band_rows, columns, 3, half_heads, HD)]
    unnamed x42 -> x13, local copies, waits for them, and re-layouts: 18.2 us -> 7.22 us
  transfers between devices with their start and end apart: 5 -> 0, of which waited for: 4 -> 0; matrix products, arithmetic and copies ran while one was open for 13% -> 0% of each run, Pallas kernels for 0% -> 0%
where the time goes in v1:
time: 88.7 us; the launch traced here: 88.4 us
  Pallas kernels  79.9 us (90%)
  local copies, waits for them, and re-layouts  7.85 us (9%)
    pallas_call x1, Pallas kernels, body(): pl.pallas_call(kernel, out_shape=(jax.ShapeDtypeStruct((RANKS, 8, D), BF)...  79.9 us
    unnamed x13, local copies, waits for them, and re-layouts  7.22 us

profile of v1, /device:TPU:1, one launch (start us, length us, event | category | flops | bytes accessed | tf_op | source)
XLA Modules:
  0.0 88.4 jit_solution(8566144588114088595)
XLA Ops:
  0.6 0.0 copy-start
  0.6 1.4 %copy-done = bf16[512,1536]{1,0:T(8,128)(2,1)S(1)} copy-done((bf16[512,1536]{1,0:T(8,128)(2,1)S(1)}, bf16[512,1536]{1,0:T(8,128)(2,1)}, u32[]{:S(2)}) %copy-start) | copy-done | bytes 1572888
  2.0 0.0 copy-start.1
  2.0 1.0 %copy-done.1 = bf16[1,1,512,512]{3,2,1,0:T(8,128)(2,1)S(1)} copy-done((bf16[1,1,512,512]{3,2,1,0:T(8,128)(2,1)S(1)}, bf16[1,1,512,512]{3,2,1,0:T(8,128)(2,1)}, u32[]{:S(2)}) %copy-start.1) | copy-done | bytes 524312
  3.1 0.0 copy-start.2
  3.1 1.0 %copy-done.2 = bf16[1,1,512,512]{3,2,1,0:T(8,128)(2,1)S(1)} copy-done((bf16[1,1,512,512]{3,2,1,0:T(8,128)(2,1)S(1)}, bf16[1,1,512,512]{3,2,1,0:T(8,128)(2,1)}, u32[]{:S(2)}) %copy-start.2) | copy-done | bytes 524312
  4.1 0.0 copy-start.3
  4.1 1.0 %copy-done.3 = bf16[512,512]{1,0:T(8,128)(2,1)S(1)} copy-done((bf16[512,512]{1,0:T(8,128)(2,1)S(1)}, bf16[512,512]{1,0:T(8,128)(2,1)}, u32[]{:S(2)}) %copy-start.3) | copy-done | bytes 524312
  5.2 0.0 copy-start.4
  5.2 0.7 copy-done.4
  5.8 79.9 %shard_map.84 = (bf16[64,8,512]{2,1,0:T(8,128)(2,1)S(1)}, f32[8,1536]{1,0:T(8,128)S(1)}, f32[8,512]{1,0:T(8,128)S(1)}, f32[8,128]{1,0:T(8,128)S(1)}) custom-call(bf16[64,8,512]{2,1,0:T(8,128)(2,1)S(1)} %bitcast.5, bf16[64,8,512]{2,1,0:T(8,128)(2,1)S(1)} %bitcast.6, f32[1,512]{1,0:T(1,128)S(1)} %bitcast.7, bf16[512,1536]{1,0:T(8,128)(2,1)S(1)} %copy-done, ...), custom_call_target="tpu_custom_call" | custom-call | tf_op jit(solution)/shard_map/pallas_call | solution.py:311
  85.8 0.6 slice_reduce_fusion
  86.4 0.8 copy.12
  87.2 0.6 copy.13
  87.8 0.6 copy.14
Async XLA Ops:
  0.6 1.4 %copy-start = (bf16[512,1536]{1,0:T(8,128)(2,1)S(1)}, bf16[512,1536]{1,0:T(8,128)(2,1)}, u32[]{:S(2)}) copy-start(bf16[512,1536]{1,0:T(8,128)(2,1)} %w_ref.1) | copy-start | bytes 4718596
  2.0 1.0 %copy-start.1 = (bf16[1,1,512,512]{3,2,1,0:T(8,128)(2,1)S(1)}, bf16[1,1,512,512]{3,2,1,0:T(8,128)(2,1)}, u32[]{:S(2)}) copy-start(bf16[1,1,512,512]{3,2,1,0:T(8,128)(2,1)} %param.5) | copy-start | bytes 1572868
  3.1 1.0 %copy-start.2 = (bf16[1,1,512,512]{3,2,1,0:T(8,128)(2,1)S(1)}, bf16[1,1,512,512]{3,2,1,0:T(8,128)(2,1)}, u32[]{:S(2)}) copy-start(bf16[1,1,512,512]{3,2,1,0:T(8,128)(2,1)} %param.9) | copy-start | bytes 1572868
  4.1 1.0 %copy-start.3 = (bf16[512,512]{1,0:T(8,128)(2,1)S(1)}, bf16[512,512]{1,0:T(8,128)(2,1)}, u32[]{:S(2)}) copy-start(bf16[512,512]{1,0:T(8,128)(2,1)} %wo_ref.1) | copy-start | bytes 1572868
  5.2 0.7 copy-start.4

commit v2 on v1

v2 whole, which is shorter than its diff:
```python
import jax
import jax.numpy as jnp
from jax import lax
from jax.experimental import pallas as pl
from jax.experimental.pallas import tpu as pltpu
from jax.sharding import PartitionSpec as P

MESH = pl.DeviceIdType.MESH
BF = jnp.bfloat16
F32 = jnp.float32
TOK = 512
D = 512
HALF = 256
HD = 64
RANKS = 64
LINE = 4
NC = 2048 + 128
PIECES = 4
CH = 128


def dot(a, b, ca, cb):
    return lax.dot_general(a, b, (((ca,), (cb,)), ((), ())), preferred_element_type=F32)


def rows8(ref, i):
    return ref[pl.ds(i * (CH // 8), CH // 8)].astype(F32).reshape(CH, D)


def norm_of(x):
    inv = lax.rsqrt(jnp.mean(x * x, -1, keepdims=True) + 1e-05)
    return inv, x * inv


def prepare_hidden(x_ref, g_ref, hid_t):
    def step(i, carry):
        _, normed = norm_of(rows8(x_ref, i))
        at = pl.multiple_of(i * CH, CH)
        hid_t[:, pl.ds(at, CH)] = (normed * g_ref[...]).T.astype(BF)
        return carry

    lax.fori_loop(0, TOK // CH, step, 0)


def project(w_ref, off, hid_t, qkv_t):
    for part in range(3):
        p = dot(w_ref[:, part * D + off : part * D + off + HALF], hid_t[...], 0, 0).astype(BF)
        if part == 0:
            p = p * BF(HD**-0.5)
        qkv_t[part * HALF : (part + 1) * HALF, :] = p


def prepare_cotangent(c_ref, wo_ref, off, cot, ga_t):
    def step(i, carry):
        at = pl.multiple_of(i * CH, CH)
        cot[pl.ds(at, CH), :] = rows8(c_ref, i).astype(BF)
        return carry

    lax.fori_loop(0, TOK // CH, step, 0)
    ga_t[...] = dot(wo_ref[off : off + HALF, :], cot[...], 1, 1).astype(BF)


def forward(is_col, qkv_t, att_t, probs):
    qb = TOK // 2

    def head(h, carry):
        at = pl.multiple_of(h * HD, HD)
        sl = pl.ds(at, HD)
        for b in range(2):
            kl = qb * (b + 1)
            qs = slice(b * qb, (b + 1) * qb)
            q = qkv_t[sl, qs]
            k = qkv_t[pl.ds(HALF + at, HD), :kl]
            v = qkv_t[pl.ds(2 * HALF + at, HD), :kl]
            s = dot(k, q, 0, 0)
            gap = (
                lax.broadcasted_iota(jnp.int32, (kl, qb), 1)
                + b * qb
                - lax.broadcasted_iota(jnp.int32, (kl, qb), 0)
            )
            allowed = gap >= 0
            if is_col:
                allowed = jnp.logical_and(allowed, jnp.bitwise_and(gap, 7) == 0)
            s = jnp.where(allowed, s, -1e30)
            e = jnp.exp(s - jnp.max(s, 0, keepdims=True))
            p = e * (1.0 / jnp.sum(e, 0, keepdims=True))
            probs[h, :kl, qs] = p
            att_t[sl, qs] = dot(v, p.astype(BF), 1, 0).astype(BF)
        return carry

    lax.fori_loop(0, HALF // HD, head, 0)


def backward(qkv_t, ga_t, att_t, probs, d_t):
    qb = TOK // 2

    def head(h, carry):
        at = pl.multiple_of(h * HD, HD)
        sl = pl.ds(at, HD)
        dk = dv = None
        for b in range(2):
            kl = qb * (b + 1)
            qs = slice(b * qb, (b + 1) * qb)
            q = qkv_t[sl, qs]
            k = qkv_t[pl.ds(HALF + at, HD), :kl]
            v = qkv_t[pl.ds(2 * HALF + at, HD), :kl]
            ga = ga_t[sl, qs]
            p = probs[h, :kl, qs]
            delta = jnp.sum(ga.astype(F32) * att_t[sl, qs].astype(F32), 0, keepdims=True)
            ds = (p * (dot(v, ga, 0, 0) - delta)).astype(BF)
            d_t[sl, qs] = (dot(k, ds, 1, 0) * (HD**-0.5)).astype(BF)
            dkb, dvb = dot(q, ds, 1, 1), dot(ga, p.astype(BF), 1, 1)
            if b == 0:
                dk, dv = dkb, dvb
            else:
                dk = jnp.concatenate([dk + dkb[:, :qb], dkb[:, qb:]], 1)
                dv = jnp.concatenate([dv + dvb[:, :qb], dvb[:, qb:]], 1)
        d_t[pl.ds(HALF + at, HD), :] = dk.astype(BF)
        d_t[pl.ds(2 * HALF + at, HD), :] = dv.astype(BF)
        return carry

    lax.fori_loop(0, HALF // HD, head, 0)


def hidden_grad(w_ref, off, d_t, dh):
    for part in range(3):
        d = d_t[part * HALF : (part + 1) * HALF, :]
        term = dot(d, w_ref[:, part * D + off : part * D + off + HALF], 0, 1)
        if part == 0:
            dh[...] = term
        else:
            dh[...] += term


def qkv_terms(hid_t, d_t, terms):
    for part in range(3):
        d = d_t[part * HALF : (part + 1) * HALF, :]
        at = part * HALF
        terms[:, :, at : at + HALF] = dot(hid_t[...], d, 1, 1).reshape(RANKS, 8, HALF)


def out_terms(off, cot, att_t, terms):
    half = slice(off // 8, (off + HALF) // 8)
    terms[half, :, 3 * HALF : 3 * HALF + D] = dot(att_t[...], cot[...], 1, 0).reshape(HALF // 8, 8, D)


def gain_term(x_ref, dh):
    def step(i, total):
        _, normed = norm_of(rows8(x_ref, i))
        at = pl.multiple_of(i * CH, CH)
        return total + jnp.sum(dh[pl.ds(at, CH), :] * normed, 0, keepdims=True)

    return lax.fori_loop(0, TOK // CH, step, jnp.zeros((1, D), F32))


def kernel(
    x_hbm, c_hbm, g_hbm, w_hbm, wo_hbm,
    out_hbm, gq_ref, go_ref, gg_ref,
    out_ref, x_ref, c_ref, g_ref, w_ref, wo_ref,
    xr, cr, hid_t, cot, qkv_t, ga_t, att_t, d_t, probs, dh_row, dh_col, dh_send, dh_recv,
    terms_a, core_send_a, core_recv_a, plane_send_a, plane_recv_a, z_sum_a, z_send_a, z_recv_a,
    terms_b, core_send_b, core_recv_b, plane_send_b, plane_recv_b, z_sum_b, z_send_b, z_recv_b,
    send_sem, recv_sem, own_sem,
):
    me = lax.axis_index("seq")
    line = lax.axis_index("dp")
    core = me % 2
    z_hi = (me // 8) % 2
    my_z = z_hi * LINE + line
    plane = (me // 16) * 4 + (me // 2) % 4
    early = (terms_a, core_send_a, core_recv_a, plane_send_a, plane_recv_a, z_sum_a, z_send_a, z_recv_a)
    late = (terms_b, core_send_b, core_recv_b, plane_send_b, plane_recv_b, z_sum_b, z_send_b, z_recv_b)

    def rank_of(other, hi):
        return (other // 4) * 16 + hi * 8 + (other % 4) * 2 + core

    def remote(src, dst, i, target):
        return pltpu.make_async_remote_copy(
            src, dst, send_sem.at[i], recv_sem.at[i], device_id=target, device_id_type=MESH
        )

    def each_peer(f):
        def step(t, carry):
            f(lax.rem(me + t, RANKS))
            return carry

        lax.fori_loop(1, RANKS, step, 0)

    loads = [
        pltpu.make_async_copy(src, dst, own_sem.at[i])
        for i, (src, dst) in enumerate(
            ((x_hbm, x_ref), (g_hbm, g_ref), (w_hbm, w_ref), (c_hbm, c_ref), (wo_hbm, wo_ref))
        )
    ]
    barrier = pltpu.get_barrier_semaphore()
    each_peer(lambda t: pl.semaphore_signal(barrier, inc=1, device_id={"seq": t}, device_id_type=MESH))
    for hi in range(2):
        for t in range(1, LINE):
            pl.semaphore_signal(
                barrier,
                inc=1,
                device_id={"seq": rank_of(plane, hi), "dp": lax.rem(line + t, LINE)},
                device_id_type=MESH,
            )
    for load in loads:
        load.start()
    pl.semaphore_wait(barrier, RANKS - 1 + 2 * (LINE - 1))

    each_peer(lambda t: remote(x_hbm.at[t], xr.at[me], 0, {"seq": t}).start())
    each_peer(lambda t: remote(c_hbm.at[t], cr.at[me], 1, {"seq": t}).start())
    for load in loads:
        load.wait()
    own_x = pltpu.make_async_copy(x_ref.at[me], xr.at[me], own_sem.at[0])
    own_c = pltpu.make_async_copy(c_ref.at[me], cr.at[me], own_sem.at[1])
    own_x.start()
    own_c.start()
    rest = pl.ds(0, RANKS - 1)
    in_x = remote(x_hbm.at[rest], xr.at[rest], 0, {"seq": me})
    in_c = remote(c_hbm.at[rest], cr.at[rest], 1, {"seq": me})

    def core_phase(bufs, i):
        terms, core_send, core_recv = bufs[:3]

        def pack(b, carry):
            core_send[b] = terms[2 * b + 1 - core].astype(BF)
            return carry

        lax.fori_loop(0, RANKS // 2, pack, 0)
        pair = remote(core_send, core_recv, i, {"seq": me + 1 - 2 * core})
        pair.start()
        return pair

    def plane_phase(bufs, i, pair):
        terms, _, core_recv, plane_send, plane_recv = bufs[:5]
        pair.wait_recv()

        def pack(b, carry):
            y, hi, x = b // 8, (b // 4) % 2, b % 4
            total = terms[2 * b + core] + core_recv[b].astype(F32)
            terms[2 * b + core] = total
            plane_send[y * 4 + x, hi] = total.astype(BF)
            return carry

        lax.fori_loop(0, RANKS // 2, pack, 0)

        def send(t, carry):
            other = lax.rem(plane + t, 16)
            remote(plane_send.at[other], plane_recv.at[plane], i, {"seq": rank_of(other, z_hi)}).start()
            return carry

        lax.fori_loop(1, 16, send, 0)
        others = pl.ds(0, 15)
        return remote(plane_send.at[others], plane_recv.at[others], i, {"seq": me})

    def z_phase(bufs, i, plane_in):
        terms, _, _, _, plane_recv, z_sum, z_send, z_recv = bufs
        plane_in.wait_recv()
        for hi in range(2):
            own = terms[rank_of(plane, hi)]

            def add(t, total, hi=hi):
                return total + plane_recv[lax.rem(plane + t, 16), hi].astype(F32)

            total = lax.fori_loop(1, 16, add, own)
            z_sum[hi] = total
            z_send[hi] = total.astype(BF)

        def send(t, carry):
            z = lax.rem(my_z + t, 2 * LINE)
            hi = z // LINE
            remote(z_send.at[hi], z_recv.at[my_z], i, {"seq": rank_of(plane, hi), "dp": z % LINE}).start()
            return carry

        lax.fori_loop(1, 2 * LINE, send, 0)
        others = pl.ds(0, 2 * LINE - 1)
        return remote(z_recv.at[others], z_recv.at[others], i, {"seq": me})

    def z_total(bufs, z_in):
        z_sum, _, z_recv = bufs[5:]
        z_in.wait_recv()

        def add(t, total):
            return total + z_recv[lax.rem(my_z + t, 2 * LINE)].astype(F32)

        return lax.fori_loop(1, 2 * LINE, add, z_sum[z_hi])

    prepare_hidden(x_ref, g_ref, hid_t)
    project(w_ref, 0, hid_t, qkv_t)
    forward(False, qkv_t, att_t, probs)
    prepare_cotangent(c_ref, wo_ref, 0, cot, ga_t)
    backward(qkv_t, ga_t, att_t, probs, d_t)
    qkv_terms(hid_t, d_t, terms_a)
    pair_a = core_phase(early, 3)
    hidden_grad(w_ref, 0, d_t, dh_row)
    out_terms(0, cot, att_t, terms_b)
    gain_row = gain_term(x_ref, dh_row)
    plane_a = plane_phase(early, 4, pair_a)

    own_x.wait()
    in_x.wait_recv()
    prepare_hidden(xr, g_ref, hid_t)
    project(w_ref, HALF, hid_t, qkv_t)
    forward(True, qkv_t, att_t, probs)
    own_c.wait()
    in_c.wait_recv()
    prepare_cotangent(cr, wo_ref, HALF, cot, ga_t)
    backward(qkv_t, ga_t, att_t, probs, d_t)
    hidden_grad(w_ref, HALF, d_t, dh_col)

    def round_out(i, carry):
        at = pl.multiple_of(i * CH, CH)
        dh_send[pl.ds(i * (CH // 8), CH // 8)] = dh_col[pl.ds(at, CH), :].reshape(CH // 8, 8, D).astype(BF)
        return carry

    lax.fori_loop(0, TOK // CH, round_out, 0)
    each_peer(lambda t: remote(dh_send.at[t], dh_recv.at[me], 2, {"seq": t}).start())
    own_h = pltpu.make_async_copy(dh_send.at[me], dh_recv.at[me], own_sem.at[0])
    own_h.start()
    out_in = remote(dh_send.at[rest], dh_recv.at[rest], 2, {"seq": me})

    qkv_terms(hid_t, d_t, terms_b)
    out_terms(HALF, cot, att_t, terms_b)
    gain = gain_row + gain_term(xr, dh_col)
    terms_b[:, :, 3 * HALF + D :] = jnp.broadcast_to(gain, (128, D)).T.reshape(RANKS, 8, 128)
    pair_b = core_phase(late, 6)
    z_a = z_phase(early, 5, plane_a)
    plane_b = plane_phase(late, 7, pair_b)

    own_h.wait()
    out_in.wait_recv()

    def finish(i, carry):
        at = pl.multiple_of(i * CH, CH)
        inv, normed = norm_of(rows8(x_ref, i))
        grad_normed = (dh_row[pl.ds(at, CH), :] + rows8(dh_recv, i)) * g_ref[...]
        mean = jnp.mean(grad_normed * normed, -1, keepdims=True)
        grad = rows8(c_ref, i) + inv * (grad_normed - normed * mean)
        out_ref[pl.ds(i * (CH // 8), CH // 8)] = grad.astype(BF).reshape(CH // 8, 8, D)
        return carry

    lax.fori_loop(0, TOK // CH, finish, 0)
    out_copy = pltpu.make_async_copy(out_ref, out_hbm, own_sem.at[1])
    out_copy.start()

    z_b = z_phase(late, 8, plane_b)
    total_a = z_total(early, z_a)
    total_b = z_total(late, z_b)
    for part in range(3):
        gq_ref[:, part * D : part * D + HALF] = total_a[:, part * HALF : (part + 1) * HALF]
        gq_ref[:, part * D + HALF : (part + 1) * D] = total_b[:, part * HALF : (part + 1) * HALF]
    go_ref[...] = total_b[:, 3 * HALF : 3 * HALF + D]
    gg_ref[...] = total_b[:, 3 * HALF + D :]

    out_copy.wait()
    for copy in (in_x, in_c, out_in, pair_a, plane_a, z_a, pair_b, plane_b, z_b):
        copy.wait_send()


def deliver(grad, gq, go, gg, grad_out, gq_out, go_out, gg_out, grad_v, gq_v, go_v, gg_v, gain, sem):
    step = RANKS // PIECES
    moves = [(gg, gg_v, gg_out), (gq, gq_v, gq_out), (go, go_v, go_out)]
    moves += [
        tuple(r.at[pl.ds(i * step, step)] for r in (grad, grad_v, grad_out)) for i in range(PIECES)
    ]
    loads = [pltpu.make_async_copy(a, b, sem.at[0, i]) for i, (a, b, _) in enumerate(moves)]
    for load in loads:
        load.start()
    stores = []
    for i, (_, b, c) in enumerate(moves):
        loads[i].wait()
        if i == 0:
            rows = lax.broadcasted_iota(jnp.int32, (8, 128), 0)
            lanes = lax.broadcasted_iota(jnp.int32, (8, 128), 1)
            gain[...] = jnp.sum(jnp.where(rows == lanes, gg_v[...], 0.0), 0, keepdims=True)[:, :8]
            b = gain
        stores.append(pltpu.make_async_copy(b, c, sem.at[1, i]))
        stores[-1].start()
    for store in stores:
        store.wait()


def sum_buffers(cols):
    return [
        pltpu.VMEM((RANKS, 8, cols), F32),
        pltpu.VMEM((RANKS // 2, 8, cols), BF),
        pltpu.VMEM((RANKS // 2, 8, cols), BF),
        pltpu.VMEM((16, 2, 8, cols), BF),
        pltpu.VMEM((16, 2, 8, cols), BF),
        pltpu.VMEM((2, 8, cols), F32),
        pltpu.VMEM((2, 8, cols), BF),
        pltpu.VMEM((2 * LINE, 8, cols), BF),
    ]


def body(inputs, norm_gain, qkv_weight, out_weight, out_cotan):
    vmem = pl.BlockSpec(memory_space=pltpu.VMEM)
    hbm = pl.BlockSpec(memory_space=pl.ANY)
    shapes = (
        jax.ShapeDtypeStruct((RANKS, 8, D), BF),
        jax.ShapeDtypeStruct((8, 3 * D), F32),
        jax.ShapeDtypeStruct((8, D), F32),
    )
    results = pl.pallas_call(
        kernel,
        out_shape=shapes + (jax.ShapeDtypeStruct((8, 128), F32),),
        in_specs=[hbm] * 5,
        out_specs=(hbm, vmem, vmem, vmem),
        scratch_shapes=[
            pltpu.VMEM((RANKS, 8, D), BF),
            pltpu.VMEM((RANKS, 8, D), BF),
            pltpu.VMEM((RANKS, 8, D), BF),
            pltpu.VMEM((1, D), F32),
            pltpu.VMEM((D, 3 * D), BF),
            pltpu.VMEM((D, D), BF),
            pltpu.VMEM((RANKS, 8, D), BF),
            pltpu.VMEM((RANKS, 8, D), BF),
            pltpu.VMEM((D, TOK), BF),
            pltpu.VMEM((TOK, D), BF),
            pltpu.VMEM((3 * HALF, TOK), BF),
            pltpu.VMEM((HALF, TOK), BF),
            pltpu.VMEM((HALF, TOK), BF),
            pltpu.VMEM((3 * HALF, TOK), BF),
            pltpu.VMEM((HALF // HD, TOK, TOK), F32),
            pltpu.VMEM((TOK, D), F32),
            pltpu.VMEM((TOK, D), F32),
            pltpu.VMEM((RANKS, 8, D), BF),
            pltpu.VMEM((RANKS, 8, D), BF),
            *sum_buffers(3 * HALF),
            *sum_buffers(3 * HALF + D + 128),
            pltpu.SemaphoreType.DMA((9,)),
            pltpu.SemaphoreType.DMA((9,)),
            pltpu.SemaphoreType.DMA((5,)),
        ],
        compiler_params=pltpu.CompilerParams(
            collective_id=0, has_side_effects=True, vmem_limit_bytes=60 * 1024 * 1024
        ),
    )(
        inputs.reshape(RANKS, 8, D),
        out_cotan.reshape(RANKS, 8, D),
        norm_gain.reshape(1, D),
        qkv_weight,
        out_weight,
    )
    grad, grad_qkv, grad_out, grad_gain = pl.pallas_call(
        deliver,
        out_shape=shapes + (jax.ShapeDtypeStruct((1, 8), F32),),
        in_specs=[hbm] * 4,
        out_specs=(hbm,) * 4,
        scratch_shapes=[
            pltpu.VMEM((RANKS, 8, D), BF),
            pltpu.VMEM((8, 3 * D), F32),
            pltpu.VMEM((8, D), F32),
            pltpu.VMEM((8, 128), F32),
            pltpu.VMEM((1, 8), F32),
            pltpu.SemaphoreType.DMA((2, 3 + PIECES)),
        ],
    )(*results)
    return (grad.reshape(inputs.shape), grad_qkv, grad_out, grad_gain.reshape(8))


def solution(mesh):
    return jax.shard_map(
        body,
        mesh=mesh,
        in_specs=(P("dp", "seq", None, None), P(), P(), P(), P("dp", "seq", None, None)),
        out_specs=(P("dp", "seq", None, None), P("seq", None), P("seq", None), P("seq")),
        check_vma=False,
    )
```

time: 88.7 us -> 72.8 us (0.82)
  local copies, waits for them, and re-layouts: 7.85 us -> 0 us
  Pallas kernels: 79.9 us -> 72.1 us
    pallas_call x1 -> x2, Pallas kernels: 79.9 us -> 72.1 us  [the longest x1 70.1 us: body(): pl.pallas_call(kernel, out_shape=shapes + (jax.ShapeDtypeStruct((8, 128),...]
    unnamed x13 -> x0, local copies, waits for them, and re-layouts: 7.22 us -> none
where the time goes in v2:
time: 72.8 us; the launch traced here: 72.7 us
  Pallas kernels  72.1 us (99%)
    pallas_call x1, Pallas kernels, body(): pl.pallas_call(kernel, out_shape=shapes + (jax.ShapeDtypeStruct((8, 128),...  70.1 us
    pallas_call x1, Pallas kernels, body(): pl.pallas_call(deliver, out_shape=shapes + (jax.ShapeDtypeStruct((1, 8),...  1.92 us

profile of v2, /device:TPU:1, one launch (start us, length us, event | category | flops | bytes accessed | tf_op | source)
XLA Modules:
  0.0 72.7 jit_solution(10768057959958663301)
XLA Ops:
  0.6 70.1 %shard_map.84 = (bf16[64,8,512]{2,1,0:T(8,128)(2,1)}, f32[8,1536]{1,0:T(8,128)}, f32[8,512]{1,0:T(8,128)}, f32[8,128]{1,0:T(8,128)}) custom-call(bf16[64,8,512]{2,1,0:T(8,128)(2,1)} %bitcast.5, bf16[64,8,512]{2,1,0:T(8,128)(2,1)} %bitcast.6, f32[1,512]{1,0:T(1,128)} %bitcast.7, bf16[512,1536]{1,0:T(8,128)(2,1)} %w_hbm.1, bf16[512,512]{1,0:T(8,128)(2,1)} %wo_hbm.1), custom_call_target="tpu_custom_call" | custom-call | tf_op jit(solution)/shard_map/pallas_call | solution.py:403
  70.8 1.9 %shard_map.85 = (bf16[64,8,512]{2,1,0:T(8,128)(2,1)}, f32[8,1536]{1,0:T(8,128)}, f32[8,512]{1,0:T(8,128)}, f32[1,8]{1,0:T(1,128)}) custom-call(bf16[64,8,512]{2,1,0:T(8,128)(2,1)} %get-tuple-element.12.grad, f32[8,1536]{1,0:T(8,128)} %get-tuple-element.13.gq, f32[8,512]{1,0:T(8,128)} %get-tuple-element.14.go, f32[8,128]{1,0:T(8,128)} %get-tuple-element.15.gg), custom_call_target="tpu_custom_call" | custom-call | tf_op jit(solution)/shard_map/pallas_call | solution.py:444

commit v3 on v2

--- a/solution.py
+++ b/solution.py
@@ -14,7 +14,6 @@
 HD = 64
 RANKS = 64
 LINE = 4
-NC = 2048 + 128
 PIECES = 4
 CH = 128
 
@@ -91,7 +90,7 @@
     lax.fori_loop(0, HALF // HD, head, 0)
 
 
-def backward(qkv_t, ga_t, att_t, probs, d_t):
+def backward(first, last, qkv_t, ga_t, att_t, probs, d_t):
     qb = TOK // 2
 
     def head(h, carry):
@@ -119,7 +118,7 @@
         d_t[pl.ds(2 * HALF + at, HD), :] = dv.astype(BF)
         return carry
 
-    lax.fori_loop(0, HALF // HD, head, 0)
+    lax.fori_loop(first, last, head, 0)
 
 
 def hidden_grad(w_ref, off, d_t, dh):
@@ -136,12 +135,12 @@
     for part in range(3):
         d = d_t[part * HALF : (part + 1) * HALF, :]
         at = part * HALF
-        terms[:, :, at : at + HALF] = dot(hid_t[...], d, 1, 1).reshape(RANKS, 8, HALF)
+        terms[:, :, :, at : at + HALF] = dot(hid_t[...], d, 1, 1).reshape(RANKS // 2, 2, 8, HALF)
 
 
 def out_terms(off, cot, att_t, terms):
-    half = slice(off // 8, (off + HALF) // 8)
-    terms[half, :, 3 * HALF : 3 * HALF + D] = dot(att_t[...], cot[...], 1, 0).reshape(HALF // 8, 8, D)
+    half = slice(off // 16, (off + HALF) // 16)
+    terms[half] = dot(att_t[...], cot[...], 1, 0).reshape(HALF // 16, 2, 8, D)
 
 
 def gain_term(x_ref, dh):
@@ -160,6 +159,8 @@
     xr, cr, hid_t, cot, qkv_t, ga_t, att_t, d_t, probs, dh_row, dh_col, dh_send, dh_recv,
     terms_a, core_send_a, core_recv_a, plane_send_a, plane_recv_a, z_sum_a, z_send_a, z_recv_a,
     terms_b, core_send_b, core_recv_b, plane_send_b, plane_recv_b, z_sum_b, z_send_b, z_recv_b,
+    terms_c, core_send_c, core_recv_c, plane_send_c, plane_recv_c, z_sum_c, z_send_c, z_recv_c,
+    gain_core, gain_pair, gain_plane, gain_planes, gain_z, gain_zs,
     send_sem, recv_sem, own_sem,
 ):
     me = lax.axis_index("seq")
@@ -169,7 +170,8 @@
     my_z = z_hi * LINE + line
     plane = (me // 16) * 4 + (me // 2) % 4
     early = (terms_a, core_send_a, core_recv_a, plane_send_a, plane_recv_a, z_sum_a, z_send_a, z_recv_a)
-    late = (terms_b, core_send_b, core_recv_b, plane_send_b, plane_recv_b, z_sum_b, z_send_b, z_recv_b)
+    middle = (terms_b, core_send_b, core_recv_b, plane_send_b, plane_recv_b, z_sum_b, z_send_b, z_recv_b)
+    late = (terms_c, core_send_c, core_recv_c, plane_send_c, plane_recv_c, z_sum_c, z_send_c, z_recv_c)
 
     def rank_of(other, hi):
         return (other // 4) * 16 + hi * 8 + (other % 4) * 2 + core
@@ -180,11 +182,12 @@
         )
 
     def each_peer(f):
-        def step(t, carry):
-            f(lax.rem(me + t, RANKS))
+        def step(i, carry):
+            for t in range(7):
+                f(lax.rem(me + 1 + i * 7 + t, RANKS))
             return carry
 
-        lax.fori_loop(1, RANKS, step, 0)
+        lax.fori_loop(0, (RANKS - 1) // 7, step, 0)
 
     loads = [
         pltpu.make_async_copy(src, dst, own_sem.at[i])
@@ -220,12 +223,7 @@
 
     def core_phase(bufs, i):
         terms, core_send, core_recv = bufs[:3]
-
-        def pack(b, carry):
-            core_send[b] = terms[2 * b + 1 - core].astype(BF)
-            return carry
-
-        lax.fori_loop(0, RANKS // 2, pack, 0)
+        core_send[...] = terms[:, 1 - core].astype(BF)
         pair = remote(core_send, core_recv, i, {"seq": me + 1 - 2 * core})
         pair.start()
         return pair
@@ -233,62 +231,70 @@
     def plane_phase(bufs, i, pair):
         terms, _, core_recv, plane_send, plane_recv = bufs[:5]
         pair.wait_recv()
-
-        def pack(b, carry):
-            y, hi, x = b // 8, (b // 4) % 2, b % 4
-            total = terms[2 * b + core] + core_recv[b].astype(F32)
-            terms[2 * b + core] = total
-            plane_send[y * 4 + x, hi] = total.astype(BF)
-            return carry
-
-        lax.fori_loop(0, RANKS // 2, pack, 0)
-
-        def send(t, carry):
+        plane_send[...] = (terms[:, core] + core_recv[...].astype(F32)).astype(BF).reshape(plane_send.shape)
+        for t in range(1, 16):
             other = lax.rem(plane + t, 16)
-            remote(plane_send.at[other], plane_recv.at[plane], i, {"seq": rank_of(other, z_hi)}).start()
-            return carry
-
-        lax.fori_loop(1, 16, send, 0)
-        others = pl.ds(0, 15)
-        return remote(plane_send.at[others], plane_recv.at[others], i, {"seq": me})
+            remote(
+                plane_send.at[other // 4, :, other % 4],
+                plane_recv.at[plane],
+                i,
+                {"seq": rank_of(other, z_hi)},
+            ).start()
+        others = plane_recv.at[pl.ds(0, 15)]
+        return remote(others, others, i, {"seq": me})
 
     def z_phase(bufs, i, plane_in):
-        terms, _, _, _, plane_recv, z_sum, z_send, z_recv = bufs
+        terms, _, core_recv, _, plane_recv, z_sum, z_send, z_recv = bufs
         plane_in.wait_recv()
         for hi in range(2):
-            own = terms[rank_of(plane, hi)]
-
-            def add(t, total, hi=hi):
-                return total + plane_recv[lax.rem(plane + t, 16), hi].astype(F32)
-
-            total = lax.fori_loop(1, 16, add, own)
+            own = rank_of(plane, hi) // 2
+            total = terms[own, core] + core_recv[own].astype(F32)
+            for t in range(1, 16):
+                total += plane_recv[lax.rem(plane + t, 16), hi].astype(F32)
             z_sum[hi] = total
             z_send[hi] = total.astype(BF)
-
-        def send(t, carry):
+        for t in range(1, 2 * LINE):
             z = lax.rem(my_z + t, 2 * LINE)
             hi = z // LINE
             remote(z_send.at[hi], z_recv.at[my_z], i, {"seq": rank_of(plane, hi), "dp": z % LINE}).start()
-            return carry
-
-        lax.fori_loop(1, 2 * LINE, send, 0)
-        others = pl.ds(0, 2 * LINE - 1)
-        return remote(z_recv.at[others], z_recv.at[others], i, {"seq": me})
+        others = z_recv.at[pl.ds(0, 2 * LINE - 1)]
+        return remote(others, others, i, {"seq": me})
 
     def z_total(bufs, z_in):
         z_sum, _, z_recv = bufs[5:]
         z_in.wait_recv()
-
-        def add(t, total):
-            return total + z_recv[lax.rem(my_z + t, 2 * LINE)].astype(F32)
-
-        return lax.fori_loop(1, 2 * LINE, add, z_sum[z_hi])
+        total = z_sum[z_hi]
+        for t in range(1, 2 * LINE):
+            total += z_recv[lax.rem(my_z + t, 2 * LINE)].astype(F32)
+        return total
+
+    def gain_plane_phase(pair):
+        pair.wait_recv()
+        gain_plane[...] = gain_core[...] + gain_pair[...]
+        for t in range(1, 16):
+            to = rank_of(lax.rem(plane + t, 16), z_hi)
+            remote(gain_plane, gain_planes.at[plane], 12, {"seq": to}).start()
+        others = gain_planes.at[pl.ds(0, 15)]
+        return remote(others, others, 12, {"seq": me})
+
+    def gain_z_phase(plane_in):
+        plane_in.wait_recv()
+        total = gain_plane[...]
+        for t in range(1, 16):
+            total += gain_planes[lax.rem(plane + t, 16)]
+        gain_z[...] = total
+        for t in range(1, 2 * LINE):
+            z = lax.rem(my_z + t, 2 * LINE)
+            to = {"seq": rank_of(plane, z // LINE), "dp": z % LINE}
+            remote(gain_z, gain_zs.at[my_z], 13, to).start()
+        others = gain_zs.at[pl.ds(0, 2 * LINE - 1)]
+        return remote(others, others, 13, {"seq": me})
 
     prepare_hidden(x_ref, g_ref, hid_t)
     project(w_ref, 0, hid_t, qkv_t)
     forward(False, qkv_t, att_t, probs)
     prepare_cotangent(c_ref, wo_ref, 0, cot, ga_t)
-    backward(qkv_t, ga_t, att_t, probs, d_t)
+    backward(0, 4, qkv_t, ga_t, att_t, probs, d_t)
     qkv_terms(hid_t, d_t, terms_a)
     pair_a = core_phase(early, 3)
     hidden_grad(w_ref, 0, d_t, dh_row)
@@ -304,7 +310,12 @@
     own_c.wait()
     in_c.wait_recv()
     prepare_cotangent(cr, wo_ref, HALF, cot, ga_t)
-    backward(qkv_t, ga_t, att_t, probs, d_t)
+    out_terms(HALF, cot, att_t, terms_b)
+    pair_b = core_phase(middle, 6)
+    z_a = z_phase(early, 5, plane_a)
+    backward(0, 2, qkv_t, ga_t, att_t, probs, d_t)
+    plane_b = plane_phase(middle, 7, pair_b)
+    backward(2, 4, qkv_t, ga_t, att_t, probs, d_t)
     hidden_grad(w_ref, HALF, d_t, dh_col)
 
     def round_out(i, carry):
@@ -318,13 +329,19 @@
     own_h.start()
     out_in = remote(dh_send.at[rest], dh_recv.at[rest], 2, {"seq": me})
 
-    qkv_terms(hid_t, d_t, terms_b)
-    out_terms(HALF, cot, att_t, terms_b)
+    qkv_terms(hid_t, d_t, terms_c)
+    pair_c = core_phase(late, 9)
     gain = gain_row + gain_term(xr, dh_col)
-    terms_b[:, :, 3 * HALF + D :] = jnp.broadcast_to(gain, (128, D)).T.reshape(RANKS, 8, 128)
-    pair_b = core_phase(late, 6)
-    z_a = z_phase(early, 5, plane_a)
-    plane_b = plane_phase(late, 7, pair_b)
+    gain_core[...] = jnp.zeros((8, 128), F32)
+    for i in range(D // 128):
+        gain_core[i : i + 1, :] = gain[:, i * 128 : (i + 1) * 128]
+    pair_g = remote(gain_core, gain_pair, 14, {"seq": me + 1 - 2 * core})
+    pair_g.start()
+    plane_c = plane_phase(late, 10, pair_c)
+    z_b = z_phase(middle, 8, plane_b)
+    plane_g = gain_plane_phase(pair_g)
+    z_c = z_phase(late, 11, plane_c)
+    z_g = gain_z_phase(plane_g)
 
     own_h.wait()
     out_in.wait_recv()
@@ -342,17 +359,26 @@
     out_copy = pltpu.make_async_copy(out_ref, out_hbm, own_sem.at[1])
     out_copy.start()
 
-    z_b = z_phase(late, 8, plane_b)
     total_a = z_total(early, z_a)
-    total_b = z_total(late, z_b)
+    go_ref[...] = z_total(middle, z_b)
+    total_c = z_total(late, z_c)
     for part in range(3):
         gq_ref[:, part * D : part * D + HALF] = total_a[:, part * HALF : (part + 1) * HALF]
-        gq_ref[:, part * D + HALF : (part + 1) * D] = total_b[:, part * HALF : (part + 1) * HALF]
-    go_ref[...] = total_b[:, 3 * HALF : 3 * HALF + D]
-    gg_ref[...] = total_b[:, 3 * HALF + D :]
+        gq_ref[:, part * D + HALF : (part + 1) * D] = total_c[:, part * HALF : (part + 1) * HALF]
+    z_g.wait_recv()
+
+    total_g = gain_z[...]
+    for t in range(1, 2 * LINE):
+        total_g += gain_zs[lax.rem(my_z + t, 2 * LINE)]
+    rows = lax.broadcasted_iota(jnp.int32, (8, 128), 0)
+    lanes = lax.broadcasted_iota(jnp.int32, (8, 128), 1)
+    mine = jnp.sum(jnp.where(rows == me // 16, total_g, 0.0), 0, keepdims=True)
+    picked = jnp.where(lanes == (me % 16) * 8 + rows, mine, 0.0)
+    gg_ref[...] = jnp.broadcast_to(jnp.sum(picked, 1, keepdims=True), (8, 128))
 
     out_copy.wait()
-    for copy in (in_x, in_c, out_in, pair_a, plane_a, z_a, pair_b, plane_b, z_b):
+    sums = (pair_a, plane_a, z_a, pair_b, plane_b, z_b, pair_c, plane_c, z_c, pair_g, plane_g, z_g)
+    for copy in (in_x, in_c, out_in, *sums):
         copy.wait_send()
 
 
@@ -381,10 +407,10 @@
 
 def sum_buffers(cols):
     return [
-        pltpu.VMEM((RANKS, 8, cols), F32),
+        pltpu.VMEM((RANKS // 2, 2, 8, cols), F32),
         pltpu.VMEM((RANKS // 2, 8, cols), BF),
         pltpu.VMEM((RANKS // 2, 8, cols), BF),
-        pltpu.VMEM((16, 2, 8, cols), BF),
+        pltpu.VMEM((4, 2, 4, 8, cols), BF),
         pltpu.VMEM((16, 2, 8, cols), BF),
         pltpu.VMEM((2, 8, cols), F32),
         pltpu.VMEM((2, 8, cols), BF),
@@ -426,9 +452,16 @@
             pltpu.VMEM((RANKS, 8, D), BF),
             pltpu.VMEM((RANKS, 8, D), BF),
             *sum_buffers(3 * HALF),
-            *sum_buffers(3 * HALF + D + 128),
-            pltpu.SemaphoreType.DMA((9,)),
-            pltpu.SemaphoreType.DMA((9,)),
+            *sum_buffers(D),
+            *sum_buffers(3 * HALF),
+            pltpu.VMEM((8, 128), F32),
+            pltpu.VMEM((8, 128), F32),
+            pltpu.VMEM((8, 128), F32),
+            pltpu.VMEM((16, 8, 128), F32),
+            pltpu.VMEM((8, 128), F32),
+            pltpu.VMEM((2 * LINE, 8, 128), F32),
+            pltpu.SemaphoreType.DMA((15,)),
+            pltpu.SemaphoreType.DMA((15,)),
             pltpu.SemaphoreType.DMA((5,)),
         ],
         compiler_params=pltpu.CompilerParams(

time: 72.8 us -> 69.7 us (0.957)
  Pallas kernels: 72.1 us -> 68.9 us
    pallas_call x1, Pallas kernels: 70.1 us -> 67 us  [body(): pl.pallas_call(kernel, out_shape=shapes + (jax.ShapeDtypeStruct((8, 128),...]
where the time goes in v3:
time: 69.7 us; the launch traced here: 69.6 us
  Pallas kernels  68.9 us (99%)
    pallas_call x1, Pallas kernels, body(): pl.pallas_call(kernel, out_shape=shapes + (jax.ShapeDtypeStruct((8, 128),...  67 us
    pallas_call x1, Pallas kernels, body(): pl.pallas_call(deliver, out_shape=shapes + (jax.ShapeDtypeStruct((1, 8),...  1.92 us

profile of v3, /device:TPU:1, one launch (start us, length us, event | category | flops | bytes accessed | tf_op | source)
XLA Modules:
  0.0 69.6 jit_solution(12732987916085453461)
XLA Ops:
  0.6 67.0 %shard_map.84 = (bf16[64,8,512]{2,1,0:T(8,128)(2,1)}, f32[8,1536]{1,0:T(8,128)}, f32[8,512]{1,0:T(8,128)}, f32[8,128]{1,0:T(8,128)}) custom-call(bf16[64,8,512]{2,1,0:T(8,128)(2,1)} %bitcast.5, bf16[64,8,512]{2,1,0:T(8,128)(2,1)} %bitcast.6, f32[1,512]{1,0:T(1,128)} %bitcast.7, bf16[512,1536]{1,0:T(8,128)(2,1)} %w_hbm.1, bf16[512,512]{1,0:T(8,128)(2,1)} %wo_hbm.1), custom_call_target="tpu_custom_call" | custom-call | tf_op jit(solution)/shard_map/pallas_call | solution.py:429
  67.6 1.9 %shard_map.85 = (bf16[64,8,512]{2,1,0:T(8,128)(2,1)}, f32[8,1536]{1,0:T(8,128)}, f32[8,512]{1,0:T(8,128)}, f32[1,8]{1,0:T(1,128)}) custom-call(bf16[64,8,512]{2,1,0:T(8,128)(2,1)} %get-tuple-element.12.grad, f32[8,1536]{1,0:T(8,128)} %get-tuple-element.13.gq, f32[8,512]{1,0:T(8,128)} %get-tuple-element.14.go, f32[8,128]{1,0:T(8,128)} %get-tuple-element.15.gg), custom_call_target="tpu_custom_call" | custom-call | tf_op jit(solution)/shard_map/pallas_call | solution.py:477

commit v4 on v3

--- a/solution.py
+++ b/solution.py
@@ -31,10 +31,13 @@
     return inv, x * inv
 
 
-def prepare_hidden(x_ref, g_ref, hid_t):
+def prepare_hidden(x_ref, g_ref, hid_t, keep=None):
     def step(i, carry):
-        _, normed = norm_of(rows8(x_ref, i))
+        inv, normed = norm_of(rows8(x_ref, i))
         at = pl.multiple_of(i * CH, CH)
+        if keep is not None:
+            keep[0][pl.ds(at, CH), :] = inv
+            keep[1][pl.ds(at, CH), :] = normed
         hid_t[:, pl.ds(at, CH)] = (normed * g_ref[...]).T.astype(BF)
         return carry
 
@@ -160,7 +163,7 @@
     terms_a, core_send_a, core_recv_a, plane_send_a, plane_recv_a, z_sum_a, z_send_a, z_recv_a,
     terms_b, core_send_b, core_recv_b, plane_send_b, plane_recv_b, z_sum_b, z_send_b, z_recv_b,
     terms_c, core_send_c, core_recv_c, plane_send_c, plane_recv_c, z_sum_c, z_send_c, z_recv_c,
-    gain_core, gain_pair, gain_plane, gain_planes, gain_z, gain_zs,
+    inv_row, normed_row, gain_core, gain_pair, gain_plane, gain_planes, gain_z, gain_zs,
     send_sem, recv_sem, own_sem,
 ):
     me = lax.axis_index("seq")
@@ -290,7 +293,7 @@
         others = gain_zs.at[pl.ds(0, 2 * LINE - 1)]
         return remote(others, others, 13, {"seq": me})
 
-    prepare_hidden(x_ref, g_ref, hid_t)
+    prepare_hidden(x_ref, g_ref, hid_t, (inv_row, normed_row))
     project(w_ref, 0, hid_t, qkv_t)
     forward(False, qkv_t, att_t, probs)
     prepare_cotangent(c_ref, wo_ref, 0, cot, ga_t)
@@ -343,27 +346,30 @@
     z_c = z_phase(late, 11, plane_c)
     z_g = gain_z_phase(plane_g)
 
+    total_a = z_total(early, z_a)
+    for part in range(3):
+        gq_ref[:, part * D : part * D + HALF] = total_a[:, part * HALF : (part + 1) * HALF]
+    go_ref[...] = z_total(middle, z_b)
+
     own_h.wait()
     out_in.wait_recv()
 
     def finish(i, carry):
         at = pl.multiple_of(i * CH, CH)
-        inv, normed = norm_of(rows8(x_ref, i))
+        inv, normed = inv_row[pl.ds(at, CH), :], normed_row[pl.ds(at, CH), :]
         grad_normed = (dh_row[pl.ds(at, CH), :] + rows8(dh_recv, i)) * g_ref[...]
         mean = jnp.mean(grad_normed * normed, -1, keepdims=True)
         grad = rows8(c_ref, i) + inv * (grad_normed - normed * mean)
-        out_ref[pl.ds(i * (CH // 8), CH // 8)] = grad.astype(BF).reshape(CH // 8, 8, D)
+        part = pl.ds(i * (CH // 8), CH // 8)
+        out_ref[part] = grad.astype(BF).reshape(CH // 8, 8, D)
+        pltpu.make_async_copy(out_ref.at[part], out_hbm.at[part], own_sem.at[1]).start()
         return carry
 
     lax.fori_loop(0, TOK // CH, finish, 0)
     out_copy = pltpu.make_async_copy(out_ref, out_hbm, own_sem.at[1])
-    out_copy.start()
-
-    total_a = z_total(early, z_a)
-    go_ref[...] = z_total(middle, z_b)
+
     total_c = z_total(late, z_c)
     for part in range(3):
-        gq_ref[:, part * D : part * D + HALF] = total_a[:, part * HALF : (part + 1) * HALF]
         gq_ref[:, part * D + HALF : (part + 1) * D] = total_c[:, part * HALF : (part + 1) * HALF]
     z_g.wait_recv()
 
@@ -454,6 +460,8 @@
             *sum_buffers(3 * HALF),
             *sum_buffers(D),
             *sum_buffers(3 * HALF),
+            pltpu.VMEM((TOK, 1), F32),
+            pltpu.VMEM((TOK, D), F32),
             pltpu.VMEM((8, 128), F32),
             pltpu.VMEM((8, 128), F32),
             pltpu.VMEM((8, 128), F32),

time: 69.7 us -> 69.8 us (level)
  no operation moved by 1% of the time
where the time goes in v4:
time: 69.8 us; the launch traced here: 69.6 us
  Pallas kernels  69 us (99%)
    pallas_call x1, Pallas kernels, body(): pl.pallas_call(kernel, out_shape=shapes + (jax.ShapeDtypeStruct((8, 128),...  67.1 us
    pallas_call x1, Pallas kernels, body(): pl.pallas_call(deliver, out_shape=shapes + (jax.ShapeDtypeStruct((1, 8),...  1.92 us

profile of v4, /device:TPU:1, one launch (start us, length us, event | category | flops | bytes accessed | tf_op | source)
XLA Modules:
  0.0 69.6 jit_solution(6066241435249412585)
XLA Ops:
  0.6 67.1 %shard_map.84 = (bf16[64,8,512]{2,1,0:T(8,128)(2,1)}, f32[8,1536]{1,0:T(8,128)}, f32[8,512]{1,0:T(8,128)}, f32[8,128]{1,0:T(8,128)}) custom-call(bf16[64,8,512]{2,1,0:T(8,128)(2,1)} %bitcast.5, bf16[64,8,512]{2,1,0:T(8,128)(2,1)} %bitcast.6, f32[1,512]{1,0:T(1,128)} %bitcast.7, bf16[512,1536]{1,0:T(8,128)(2,1)} %w_hbm.1, bf16[512,512]{1,0:T(8,128)(2,1)} %wo_hbm.1), custom_call_target="tpu_custom_call" | custom-call | tf_op jit(solution)/shard_map/pallas_call | solution.py:435
  67.7 1.9 %shard_map.85 = (bf16[64,8,512]{2,1,0:T(8,128)(2,1)}, f32[8,1536]{1,0:T(8,128)}, f32[8,512]{1,0:T(8,128)}, f32[1,8]{1,0:T(1,128)}) custom-call(bf16[64,8,512]{2,1,0:T(8,128)(2,1)} %get-tuple-element.12.grad, f32[8,1536]{1,0:T(8,128)} %get-tuple-element.13.gq, f32[8,512]{1,0:T(8,128)} %get-tuple-element.14.go, f32[8,128]{1,0:T(8,128)} %get-tuple-element.15.gg), custom_call_target="tpu_custom_call" | custom-call | tf_op jit(solution)/shard_map/pallas_call | solution.py:485

commit v5 on v4

--- a/solution.py
+++ b/solution.py
@@ -316,9 +316,9 @@
     out_terms(HALF, cot, att_t, terms_b)
     pair_b = core_phase(middle, 6)
     z_a = z_phase(early, 5, plane_a)
-    backward(0, 2, qkv_t, ga_t, att_t, probs, d_t)
+    backward(0, 1, qkv_t, ga_t, att_t, probs, d_t)
     plane_b = plane_phase(middle, 7, pair_b)
-    backward(2, 4, qkv_t, ga_t, att_t, probs, d_t)
+    backward(1, 4, qkv_t, ga_t, att_t, probs, d_t)
     hidden_grad(w_ref, HALF, d_t, dh_col)
 
     def round_out(i, carry):

time: 69.8 us -> 69.7 us (level)
  no operation moved by 1% of the time
where the time goes in v5:
time: 69.7 us; the launch traced here: 69.5 us
  Pallas kernels  68.9 us (99%)
    pallas_call x1, Pallas kernels, body(): pl.pallas_call(kernel, out_shape=shapes + (jax.ShapeDtypeStruct((8, 128),...  67 us
    pallas_call x1, Pallas kernels, body(): pl.pallas_call(deliver, out_shape=shapes + (jax.ShapeDtypeStruct((1, 8),...  1.92 us

profile of v5, /device:TPU:1, one launch (start us, length us, event | category | flops | bytes accessed | tf_op | source)
XLA Modules:
  0.0 69.5 jit_solution(10186538190218975087)
XLA Ops:
  0.6 67.0 %shard_map.84 = (bf16[64,8,512]{2,1,0:T(8,128)(2,1)}, f32[8,1536]{1,0:T(8,128)}, f32[8,512]{1,0:T(8,128)}, f32[8,128]{1,0:T(8,128)}) custom-call(bf16[64,8,512]{2,1,0:T(8,128)(2,1)} %bitcast.5, bf16[64,8,512]{2,1,0:T(8,128)(2,1)} %bitcast.6, f32[1,512]{1,0:T(1,128)} %bitcast.7, bf16[512,1536]{1,0:T(8,128)(2,1)} %w_hbm.1, bf16[512,512]{1,0:T(8,128)(2,1)} %wo_hbm.1), custom_call_target="tpu_custom_call" | custom-call | tf_op jit(solution)/shard_map/pallas_call | solution.py:435
  67.6 1.9 %shard_map.85 = (bf16[64,8,512]{2,1,0:T(8,128)(2,1)}, f32[8,1536]{1,0:T(8,128)}, f32[8,512]{1,0:T(8,128)}, f32[1,8]{1,0:T(1,128)}) custom-call(bf16[64,8,512]{2,1,0:T(8,128)(2,1)} %get-tuple-element.12.grad, f32[8,1536]{1,0:T(8,128)} %get-tuple-element.13.gq, f32[8,512]{1,0:T(8,128)} %get-tuple-element.14.go, f32[8,128]{1,0:T(8,128)} %get-tuple-element.15.gg), custom_call_target="tpu_custom_call" | custom-call | tf_op jit(solution)/shard_map/pallas_call | solution.py:485
